TPU v7x, 32 devices: a whole 2x2x4 slice. The times are simulated.
32 devices in a mesh: sec: 8 (over y, x, core), term: 4 (over z).
Axes of the slice: x: 2, y: 2, z: 4, core: 2. Of those that a mesh axis runs over, the one named last changes fastest.
Arguments:
- meet_env: bfloat16 [8, 24, 256, 256], P('sec', 'term'), may hold values from -0.375 to 0.375
- meet_iso: bfloat16 [8, 256, 2, 256], P('sec'), may hold values from -0.3125 to 0.3125
- last_site: bfloat16 [8, 256, 2, 256], P('sec'), may hold values from -60 to 60
- first_site: bfloat16 [8, 256, 2, 256], P('sec'), may hold values from -0.375 to 0.375
- term_kind: int32 [24, 2], P('term'), may hold values from 0 to 3
Outputs:
- two_site_out: float32 [8, 256, 2, 2, 256], P('sec')
All inputs are finite; a program needn't handle non-finite values.
Results may differ from a plain program's by a relative error of at most 0.013.
Values may be sent and summed in bfloat16 or wider, within the bound.
A program may use at most 64 MiB of HBM per device.

v0:
```python
import jax
import jax.numpy as jnp
import numpy as np
from jax import lax
from jax.sharding import PartitionSpec as P

PHYS = 2
STEPS = 2


operator_table = np.array(
    [
        [[1.0, 0.0], [0.0, 1.0]],
        [[0.0, 1.0], [1.0, 0.0]],
        [[1.0, 0.0], [0.0, -1.0]],
        [[0.0, 1.0], [-1.0, 0.0]],
    ],
    dtype=np.float32,
)
step_size = 0.2
epsilon = 1e-06


def swapped(value, axis, bit):
    mask = 2**bit
    pairs = [(source, source ^ mask) for source in range(lax.axis_size(axis))]
    return lax.ppermute(value, axis, pairs)


def shifted(block, axis, distance):
    devices = range(lax.axis_size(axis))
    route = [((i - distance) % len(devices), i) for i in devices]
    return lax.ppermute(block, axis, route)


def operator_pairs(term_kind):
    levels = jnp.arange(4, dtype=jnp.int32)
    onehot = (term_kind[:, :, None] == levels).astype(jnp.float32)
    return jnp.einsum("kjo,oxy->kjxy", onehot, jnp.asarray(operator_table, dtype=jnp.float32))


def reverse_bond(basis):
    return jnp.transpose(basis, (2, 1, 0))


def extend(environment, basis, operators):
    group_terms, bond_dim = (environment.shape[0], environment.shape[1])
    wide = jnp.dot(
        environment.reshape(group_terms * bond_dim, bond_dim),
        basis.reshape(bond_dim, 2 * bond_dim),
        preferred_element_type=jnp.float32,
    )
    wide = wide.astype(jnp.bfloat16).reshape(group_terms, bond_dim, 2, bond_dim)
    mixed = jnp.einsum(
        "kst,katm->kasm", operators.astype(jnp.bfloat16), wide, preferred_element_type=jnp.float32
    ).astype(jnp.bfloat16)
    return jnp.einsum("asm,kasn->kmn", basis, mixed, preferred_element_type=jnp.float32).astype(
        jnp.bfloat16
    )


def extend_twice(environment, first_basis, second_basis, operators):
    return extend(extend(environment, first_basis, operators), second_basis, operators)


def apply_local(vector, left_env, right_env, operators):
    pair_ops = jnp.einsum("ksx,kty->kstxy", operators[:, 0], operators[:, 1]).reshape(
        operators.shape[0], 4, 4
    )
    permuted = jnp.einsum(
        "kxy,ayc->kaxc", pair_ops.astype(jnp.bfloat16), vector, preferred_element_type=jnp.float32
    ).astype(jnp.bfloat16)
    left_applied = jnp.einsum(
        "kab,kbxc->kaxc", left_env, permuted, preferred_element_type=jnp.float32
    ).astype(jnp.bfloat16)
    return jnp.einsum("kaxc,kdc->axd", left_applied, right_env, preferred_element_type=jnp.float32)


def shards(meet_env, meet_iso, last_site, first_site, term_kind):
    own_env = meet_env[0]
    own_iso = meet_iso[0]
    own_last = last_site[0]
    own_first = first_site[0]
    bond_dim = own_env.shape[1]
    operators = operator_pairs(term_kind)
    odd_section = lax.axis_index("sec") % 2 == 1
    partner_env, partner_iso = swapped((own_env, own_iso), "sec", 0)
    first_basis = jnp.where(odd_section, partner_iso, reverse_bond(partner_iso))
    second_basis = jnp.where(odd_section, own_iso, reverse_bond(own_iso))
    chain_ops = jnp.where(odd_section, operators[:, 0], operators[:, 1])
    fresh_env = extend_twice(partner_env, first_basis, second_basis, chain_ops)
    came_env, came_site = shifted((fresh_env, own_last), "sec", 1)
    left_env = jnp.where(odd_section, partner_env, came_env)
    right_env = jnp.where(odd_section, own_env, fresh_env)
    two_site = jnp.dot(
        came_site.reshape(2 * bond_dim, bond_dim),
        own_first.reshape(bond_dim, 2 * bond_dim),
        preferred_element_type=jnp.float32,
    ).reshape(bond_dim, 4, bond_dim)
    for step_index in range(STEPS):
        partial_sum = apply_local(two_site.astype(jnp.bfloat16), left_env, right_env, operators)
        two_site = two_site - step_size * lax.psum(partial_sum.astype(jnp.bfloat16), "term").astype(
            jnp.float32
        )
    result = two_site * lax.rsqrt(jnp.mean(two_site * two_site) + epsilon)
    return result.reshape(1, bond_dim, PHYS, PHYS, bond_dim)


def solution(mesh):
    in_specs = (
        P("sec", "term", None, None),
        P("sec", None, None, None),
        P("sec", None, None, None),
        P("sec", None, None, None),
        P("term", None),
    )
    out_specs = P("sec", None, None, None, None)
    return jax.shard_map(shards, mesh=mesh, in_specs=in_specs, out_specs=out_specs, check_vma=False)
```

profile of v0, /device:TPU:0, one launch (start us, length us, event | category | flops | bytes accessed | tf_op | source)
XLA Modules:
  0.0 148.5 jit_solution(2980411247509285753)
XLA Ops:
  6.5 1.3 copy.30
  8.5 1.4 copy.29
  9.9 2.7 %collective-permute-start.1 = (bf16[6,256,256]{1,2,0:T(8,128)(2,1)S(1)}, bf16[6,256,256]{1,2,0:T(8,128)(2,1)}, u32[]{:S(2)}, u32[]{:S(2)}) collective-permute-start(bf16[6,256,256]{1,2,0:T(8,128)(2,1)S(1)} %bitcast.126), channel_id=1, source_target_pairs={{0,4},{4,0},{8,12},{12,8},{16,20},{20,16},{24,28},{28,24},{1,5},{5... | collective-permute-start | bytes 2359304 | tf_op jit(solution)/shard_map/ppermute | solution.py:27
  13.2 0.7 copy.73
  14.8 0.9 copy.36
  15.7 1.4 copy.32
  17.1 0.6 fusion.8
  17.7 0.7 copy.33
  18.9 1.8 %fusion.21 = bf16[6,256,2,256]{3,2,1,0:T(2,128)(2,1)S(1)} fusion(bf16[6,256,2,256]{3,2,1,0:T(2,128)(2,1)S(1)} %reshape.37, bf16[6,2,2,1]{2,1,3,0:T(2,128)(2,1)S(1)} %copy.51), kind=kOutput, calls=%fused_computation.21 | convolution fusion | flops 3932160 | bytes 3145776 | tf_op jit(solution)/shard_map/kst,katm->kasm/dot_general | solution.py:54
  20.7 0.6 bitcast_convert_fusion.1
  21.3 0.6 convolution_convert_fusion
  22.3 1.8 %fusion.22 = bf16[6,256,2,256]{3,2,1,0:T(2,128)(2,1)S(1)} fusion(bf16[6,256,2,256]{3,2,1,0:T(2,128)(2,1)S(1)} %reshape.40, bf16[6,2,2,1]{2,1,3,0:T(2,128)(2,1)S(1)} %copy.51), kind=kOutput, calls=%fused_computation.22 | convolution fusion | flops 3932160 | bytes 3145776 | tf_op jit(solution)/shard_map/kst,katm->kasm/dot_general | solution.py:54
  24.1 1.5 %fusion.37 = bf16[6,256,256]{1,2,0:T(8,128)(2,1)} fusion(bf16[6,256,2,256]{3,2,1,0:T(2,128)(2,1)S(1)} %fusion.22, bf16[256,2,256]{2,1,0:T(2,128)(2,1)S(1)} %copy-done.4), kind=kOutput, calls=%fused_computation.25 | convolution fusion | flops 403046400 | bytes 2621440 | tf_op jit(solution)/shard_map/asm,kasn->kmn/dot_general | solution.py:57
  25.6 1.1 reshape.33
  27.3 3.2 %convert_bitcast_fusion.1 = bf16[6,256,4,256]{3,0,2,1:T(8,128)(2,1)} fusion(bf16[6,4,4,1]{0,2,1,3:T(4,128)(2,1)S(1)} %bitcast.129, bf16[256,4,256,1]{2,1,0,3:T(4,128)(2,1)S(1)} %reshape.50), kind=kOutput, calls=%fused_computation.1 | convolution fusion | flops 14155776 | bytes 3670208 | tf_op jit(solution)/shard_map/kxy,ayc->kaxc/dot_general | solution.py:70
  30.6 7.6 %collective-permute-done.3 = bf16[6,256,256]{1,2,0:T(8,128)(2,1)} collective-permute-done((bf16[6,256,256]{1,2,0:T(8,128)(2,1)}, bf16[6,256,256]{1,2,0:T(8,128)(2,1)}, u32[]{:S(2)}, u32[]{:S(2)}) %collective-permute-start.3) | collective-permute-done | bytes 786464 | tf_op jit(solution)/shard_map/ppermute | solution.py:33
  38.2 8.2 %fusion.45 = bf16[256,4,256]{2,0,1:T(8,128)(2,1)} fusion(bf16[6,256,4,256]{3,0,2,1:T(8,128)(2,1)} %convert_bitcast_fusion.1, bf16[6,256,256]{1,2,0:T(8,128)(2,1)} %collective-permute-done.1, bf16[6,256,256]{1,2,0:T(8,128)(2,1)} %collective-permute-done.3, pred[]{:T(512)S(6)} %eq.18, bf16[6,256,256]{1,2,0:T(8,128)(2,1)} %fusion.37, ...), kind=kOutput, calls=%fused_computation.27 | convolution fusion | flops 1613234176 | bytes 6815745 | tf_op jit(solution)/shard_map/kaxc,kdc->axd/dot_general | solution.py:76
  47.2 38.2 %all-reduce.3.cloned.1.call-done = bf16[256,4,256]{2,0,1:T(8,128)(2,1)} async-done(((bf16[256,4,256]{2,0,1:T(8,128)(2,1)}), bf16[256,4,256]{2,0,1:T(8,128)(2,1)}) %all-reduce.3.cloned.1.call-update) | async-done | bytes 524304 | tf_op jit(solution)/shard_map/psum | solution.py:102
  85.4 1.3 convert_bitcast_fusion.2
  86.7 3.3 %convert_bitcast_fusion = bf16[6,256,4,256]{3,0,2,1:T(8,128)(2,1)} fusion(bf16[6,4,4,1]{0,2,1,3:T(4,128)(2,1)S(1)} %bitcast.130, bf16[256,4,256,1]{2,0,1,3:T(8,128)(2,1)S(1)} %convert_bitcast_fusion.2), kind=kOutput, calls=%fused_computation | convolution fusion | flops 14155776 | bytes 3670208 | tf_op jit(solution)/shard_map/kxy,ayc->kaxc/dot_general | solution.py:70
  90.0 8.3 %fusion.40 = bf16[256,4,256]{2,0,1:T(8,128)(2,1)} fusion(bf16[6,256,4,256]{3,0,2,1:T(8,128)(2,1)} %convert_bitcast_fusion, bf16[6,256,256]{1,2,0:T(8,128)(2,1)} %collective-permute-done.1, bf16[6,256,256]{1,2,0:T(8,128)(2,1)} %collective-permute-done.3, pred[]{:T(512)S(6)} %eq.18, bf16[6,256,256]{1,2,0:T(8,128)(2,1)} %fusion.37, ...), kind=kOutput, calls=%fused_computation.26 | convolution fusion | flops 1613234176 | bytes 6815745 | tf_op jit(solution)/shard_map/kaxc,kdc->axd/dot_general | solution.py:76
  98.3 38.5 %all-reduce.5.cloned.1.call-done = bf16[256,4,256]{2,0,1:T(8,128)(2,1)} async-done(((bf16[256,4,256]{2,0,1:T(8,128)(2,1)}), bf16[256,4,256]{2,0,1:T(8,128)(2,1)}) %all-reduce.5.cloned.1.call-update) | async-done | bytes 524304 | tf_op jit(solution)/shard_map/psum | solution.py:102
  136.8 2.0 %multiply_reduce_fusion = f32[]{:T(128)} fusion(bf16[256,4,256]{2,0,1:T(8,128)(2,1)} %all-reduce.5.cloned.1.call-done, bf16[256,4,256]{2,0,1:T(8,128)(2,1)S(1)} %copy-done, f32[256,4,256]{2,1,0:T(4,128)S(1)} %reshape.34), kind=kLoop, calls=%fused_computation.29 | loop fusion | flops 2097151 | bytes 2097156 | tf_op jit(solution)/shard_map/reduce_sum | solution.py:105
  139.9 1.8 %copy.49 = f32[1,256,2,2,256]{4,3,2,1,0:T(2,128)} copy(f32[1,256,2,2,256]{4,1,3,2,0:T(8,128)S(1)} %bitcast.118) | data formatting | bytes 2097152 | tf_op jit(solution)/shard_map/reshape | solution.py:106
  (50 shorter events, 4.7 us)
Async XLA Ops:
  6.5 6.3 %copy-start.11 = (bf16[4,2,2,1]{0,2,1,3:T(2,128)(2,1)S(1)}, bf16[4,2,2,1]{0,2,1,3:T(2,128)(2,1)}, u32[]{:S(2)}) copy-start(bf16[4,2,2,1]{0,2,1,3:T(2,128)(2,1)} %constant.67) | copy-start | bytes 100
  6.5 6.1 %copy-start.2 = (bf16[1,256,2,256]{3,2,1,0:T(2,128)(2,1)S(1)}, bf16[1,256,2,256]{3,2,1,0:T(2,128)(2,1)}, u32[]{:S(2)}) copy-start(bf16[1,256,2,256]{3,2,1,0:T(2,128)(2,1)} %param.7) | copy-start | bytes 786436
  6.5 6.4 %copy-start.10 = (s32[6,2]{0,1:T(2,128)S(1)}, s32[6,2]{0,1:T(2,128)}, u32[]{:S(2)}) copy-start(s32[6,2]{0,1:T(2,128)} %param.10) | copy-start | bytes 148
  6.5 78.9 %all-reduce.3.cloned.1.call-start = ((), (), s32[]{:S(2)}) async-start(), calls=%async_computation | async-start | bytes 1048576 | tf_op jit(solution)/shard_map/psum | solution.py:102
  7.9 5.3 %copy-start.8 = (bf16[1,256,2,256]{3,2,1,0:T(2,128)(2,1)S(1)}, bf16[1,256,2,256]{3,2,1,0:T(2,128)(2,1)}, u32[]{:S(2)}) copy-start(bf16[1,256,2,256]{3,2,1,0:T(2,128)(2,1)} %param.9) | copy-start | bytes 786436
  7.9 6.0 %collective-permute-start.2 = (bf16[256,2,256]{0,1,2:T(2,128)(2,1)S(1)}, bf16[256,2,256]{0,1,2:T(2,128)(2,1)S(1)}, u32[]{:S(2)}, u32[]{:S(2)}) collective-permute-start(bf16[256,2,256]{0,1,2:T(2,128)(2,1)S(1)} %copy.30), channel_id=1, source_target_pairs={{0,4},{4,0},{8,12},{12,8},{16,20},{20,16},{24,28},{28,24},{1,5},{5... | collective-permute-start | bytes 786440 | tf_op jit(solution)/shard_map/ppermute | solution.py:27
  8.5 17.2 %collective-permute-start = (bf16[256,2,256]{2,1,0:T(2,128)(2,1)}, bf16[256,2,256]{2,1,0:T(2,128)(2,1)}, u32[]{:S(2)}, u32[]{:S(2)}) collective-permute-start(bf16[256,2,256]{2,1,0:T(2,128)(2,1)} %bitcast.131), channel_id=1, source_target_pairs={{28,0},{0,4},{4,8},{8,12},{12,16},{16,20},{20,24},{24,28},{29,1},{... | collective-permute-start | bytes 786440 | tf_op jit(solution)/shard_map/ppermute | solution.py:33
  9.9 4.8 %copy-start.6 = (bf16[1,6,256,256]{2,3,1,0:T(8,128)(2,1)}, bf16[1,6,256,256]{2,3,1,0:T(8,128)(2,1)S(1)}, u32[]{:S(2)}) copy-start(bf16[1,6,256,256]{2,3,1,0:T(8,128)(2,1)S(1)} %copy.29) | copy-start | bytes 2359300
  9.9 5.7 %collective-permute-start.1 = (bf16[6,256,256]{1,2,0:T(8,128)(2,1)S(1)}, bf16[6,256,256]{1,2,0:T(8,128)(2,1)}, u32[]{:S(2)}, u32[]{:S(2)}) collective-permute-start(bf16[6,256,256]{1,2,0:T(8,128)(2,1)S(1)} %bitcast.126), channel_id=1, source_target_pairs={{0,4},{4,0},{8,12},{12,8},{16,20},{20,16},{24,28},{28,24},{1,5},{5... | collective-permute-start | bytes 2359304 | tf_op jit(solution)/shard_map/ppermute | solution.py:27
  12.9 2.8 %copy-start.3 = (bf16[256,2,256]{2,1,0:T(2,128)(2,1)}, bf16[256,2,256]{2,1,0:T(2,128)(2,1)S(1)}, u32[]{:S(2)}) copy-start(bf16[256,2,256]{2,1,0:T(2,128)(2,1)S(1)} %broadcast_select_fusion.2) | copy-start | bytes 786436
  18.9 1.8 %copy-start.9 = (bf16[256,2,256]{0,2,1:T(8,128)(2,1)S(1)}, bf16[256,2,256]{0,2,1:T(8,128)(2,1)}, u32[]{:S(2)}) copy-start(bf16[256,2,256]{0,2,1:T(8,128)(2,1)} %copy.36) | copy-start | bytes 786436
  22.3 1.8 %copy-start.4 = (bf16[256,2,256]{2,1,0:T(2,128)(2,1)S(1)}, bf16[256,2,256]{2,1,0:T(2,128)(2,1)}, u32[]{:S(2)}) copy-start(bf16[256,2,256]{2,1,0:T(2,128)(2,1)} %copy-done.3) | copy-start | bytes 786436
  24.1 2.6 %copy-start.5 = (bf16[32,8,2,256]{3,1,2,0:T(8,128)(2,1)S(1)}, bf16[32,8,2,256]{3,1,2,0:T(8,128)(2,1)}, u32[]{:S(2)}) copy-start(bf16[32,8,2,256]{3,1,2,0:T(8,128)(2,1)} %copy.73) | copy-start | bytes 786436
  25.6 12.6 %collective-permute-start.3 = (bf16[6,256,256]{1,2,0:T(8,128)(2,1)}, bf16[6,256,256]{1,2,0:T(8,128)(2,1)}, u32[]{:S(2)}, u32[]{:S(2)}) collective-permute-start(bf16[6,256,256]{1,2,0:T(8,128)(2,1)} %fusion.37), channel_id=1, source_target_pairs={{28,0},{0,4},{4,8},{8,12},{12,16},{16,20},{20,24},{24,28},{29,1},{... | collective-permute-start | bytes 2359304 | tf_op jit(solution)/shard_map/ppermute | solution.py:33
  27.3 10.9 %copy-start.7 = (bf16[1,6,256,256]{2,3,1,0:T(8,128)(2,1)S(1)}, bf16[1,6,256,256]{2,3,1,0:T(8,128)(2,1)}, u32[]{:S(2)}) copy-start(bf16[1,6,256,256]{2,3,1,0:T(8,128)(2,1)} %copy-done.6) | copy-start | bytes 2359300
  46.5 90.3 %all-reduce.5.cloned.1.call-start = ((), (), s32[]{:S(2)}) async-start(), calls=%async_computation.1 | async-start | bytes 1048576 | tf_op jit(solution)/shard_map/psum | solution.py:102
  90.0 46.8 %copy-start = (bf16[256,4,256]{2,0,1:T(8,128)(2,1)S(1)}, bf16[256,4,256]{2,0,1:T(8,128)(2,1)}, u32[]{:S(2)}) copy-start(bf16[256,4,256]{2,0,1:T(8,128)(2,1)} %all-reduce.3.cloned.1.call-done) | copy-start | bytes 1572868
  136.8 2.7 %copy-start.1 = (bf16[256,4,256]{2,0,1:T(8,128)(2,1)S(1)}, bf16[256,4,256]{2,0,1:T(8,128)(2,1)}, u32[]{:S(2)}) copy-start(bf16[256,4,256]{2,0,1:T(8,128)(2,1)} %all-reduce.5.cloned.1.call-done) | copy-start | bytes 1572868
Sparse Core Ops, SparseCore 0:
  46.6 38.8 all-reduce.2
  98.4 38.3 all-reduce.4
where the time goes:
time: 149 us; the launch traced here: 148 us
  waiting for transfers between devices  84.3 us (57%)
  matrix products  30.2 us (20%)
  between operations  14.4 us (10%)
  local copies, waits for them, and re-layouts  11.7 us (8%)
  other arithmetic  4.21 us (3%)
  starting transfers between devices  3.58 us (2%)
    psum x2, waiting for transfers between devices, shards(): lax.psum(partial_sum.astype(jnp.bfloat16), 'term').astype(jnp.float32)  76.7 us
    dot_general x2, matrix products, apply_local(): jnp.einsum('kaxc,kdc->axd', left_applied, right_env, preferred_element_ty...  16.5 us
    ppermute x2, waiting for transfers between devices, shifted(): return lax.ppermute(block, axis, route)  7.62 us
    dot_general x2, matrix products, apply_local(): jnp.einsum('kxy,ayc->kaxc', pair_ops.astype(jnp.bfloat16), vector, prefer...  6.52 us
    dot_general x2, matrix products, extend(): jnp.einsum('kst,katm->kasm', operators.astype(jnp.bfloat16), wide, prefer...  3.54 us
    ppermute x2, starting transfers between devices, swapped(): return lax.ppermute(value, axis, pairs)  3.21 us
  transfers between devices with their start and end apart: 6, of which 3 were waited for; matrix products, arithmetic and copies ran while one was open for 13% of the time, Pallas kernels for 0%

commit v1 on v0

v1 whole, which is shorter than its diff:
```python
import functools

import jax
import jax.numpy as jnp
from jax import lax
from jax.experimental import pallas as pl
from jax.experimental.pallas import tpu as pltpu
from jax.sharding import PartitionSpec as P

PHYS = 2
STEPS = 2
step_size = 0.2
epsilon = 1e-06
F32 = jnp.float32
BF16 = jnp.bfloat16
MESH = pl.DeviceIdType.MESH


def matmul(lhs, rhs):
    return jnp.dot(lhs, rhs, preferred_element_type=F32)


def kernel(
    n_sec,
    n_term,
    terms,
    kind_ref,
    env_ref,
    iso_ref,
    last_ref,
    first_ref,
    out_ref,
    envbuf,
    rbuf,
    fresh,
    piso,
    came,
    basis,
    table,
    g,
    v,
    two_site,
    acc,
    tot,
    recv,
    one_send,
    one_recv,
    env_send,
    env_recv,
    fresh_send,
    fresh_recv,
    in_send,
    chunk_recv,
    out_send,
):
    pairs = PHYS * PHYS
    sec = lax.axis_index("sec")
    term = lax.axis_index("term")
    odd = lax.rem(sec, 2)
    is_odd = odd == 1
    is_even = odd == 0
    partner = sec + 1 - 2 * odd
    following = lax.rem(sec + 1, n_sec)
    before = lax.rem(sec + n_sec - 1, n_sec)
    half = n_term // 2
    left_side = term < half
    inward = jnp.where(left_side, term + 1, term - 1)
    outward = jnp.where(left_side, term - 1, term + 1)
    has_outward = jnp.logical_and(term > 0, term < n_term - 1)
    middle = jnp.logical_or(term == half - 1, term == half)
    in_slot = jnp.where(middle, 1, 0)

    def at(s, t):
        return dict(device_id=(s, t), device_id_type=MESH)

    barrier = pltpu.get_barrier_semaphore()
    for s in (following, before):
        pl.semaphore_signal(barrier, inc=1, **at(s, term))
    pl.semaphore_signal(barrier, inc=1, **at(sec, inward))

    @pl.when(has_outward)
    def _():
        pl.semaphore_signal(barrier, inc=1, **at(sec, outward))
        pl.semaphore_wait(barrier, 4)

    @pl.when(jnp.logical_not(has_outward))
    def _():
        pl.semaphore_wait(barrier, 3)

    def remote(src, dst, send, receive, s, t):
        return pltpu.make_async_remote_copy(
            src_ref=src, dst_ref=dst, send_sem=send, recv_sem=receive, **at(s, t)
        )

    iso_copy = remote(iso_ref, piso, one_send.at[0], one_recv.at[0], partner, term)
    last_copy = remote(last_ref, came, one_send.at[1], one_recv.at[1], following, term)

    def env_copy(k):
        return remote(
            env_ref.at[k], envbuf.at[odd, k], env_send.at[k], env_recv.at[k], partner, term
        )

    def fresh_copy(k):
        return remote(
            fresh.at[k], envbuf.at[0, k], fresh_send.at[k], fresh_recv.at[k], following, term
        )

    def in_copy(n, x):
        return remote(
            acc.at[n, x],
            recv.at[n, in_slot, x],
            in_send.at[n, x],
            chunk_recv.at[n, in_slot, x],
            sec,
            inward,
        )

    def out_copy(n, x):
        return remote(
            tot.at[n, x],
            recv.at[n, 1, x],
            out_send.at[n, x],
            chunk_recv.at[n, 1, x],
            sec,
            outward,
        )

    def arrived(n, slot, x):
        return remote(
            acc.at[n, x],
            recv.at[n, slot, x],
            in_send.at[n, x],
            chunk_recv.at[n, slot, x],
            sec,
            inward,
        )

    iso_copy.start()
    for k in range(terms):
        env_copy(k).start()
    last_copy.start()

    def set_basis(which, source):
        @pl.when(is_odd)
        def _():
            for s in range(PHYS):
                value = source[s]
                turned = value.T
                basis[which, s] = value
                table[which, s] = turned
                if s == 1:
                    table[which, 2] = -turned

        @pl.when(is_even)
        def _():
            for s in range(PHYS):
                value = source[s]
                basis[which, s] = value.T
                table[which, s] = value
                if s == 1:
                    table[which, 2] = -value

    set_basis(1, iso_ref)

    @pl.when(is_odd)
    def _():
        def turn(k, carry):
            rbuf[k] = env_ref[k].T
            return carry

        lax.fori_loop(0, terms, turn, 0)

    iso_copy.wait_recv()
    set_basis(0, piso)

    def extend(value, which, kind):
        first = jnp.where(kind == 1, 1, jnp.where(kind == 3, 2, 0))
        second = jnp.where(kind == 0, 1, jnp.where(kind == 2, 2, 0))
        wide_0 = matmul(value, basis[which, 0]).astype(BF16)
        wide_1 = matmul(value, basis[which, 1]).astype(BF16)
        result = matmul(table[which, first], wide_0) + matmul(table[which, second], wide_1)
        return result.astype(BF16)

    def extend_term(k, carry):
        env_copy(k).wait_recv()
        kind = kind_ref[k, 1 - odd]
        value = extend(extend(envbuf[1 - odd, k], 0, kind), 1, kind)

        @pl.when(is_odd)
        def _():
            fresh[k] = value
            fresh_copy(k).start()

        @pl.when(is_even)
        def _():
            rbuf[k] = value.T

        return carry

    lax.fori_loop(0, terms, extend_term, 0)

    last_copy.wait_recv()
    for s in range(PHYS):
        for t in range(PHYS):
            value = matmul(came[s], first_ref[t])
            two_site[PHYS * s + t] = value
            v[PHYS * s + t] = value.astype(BF16)

    def left_term(k, carry):
        @pl.when(is_even)
        def _():
            fresh_copy(k).wait_recv()

        value = envbuf[0, k]
        for x in range(pairs):
            g[k, x] = matmul(value, v[x]).astype(BF16)
        return carry

    lax.fori_loop(0, terms, left_term, 0)

    for n in range(STEPS):

        def right_pair(x, carry):
            s = x // PHYS
            t = lax.rem(x, PHYS)
            total = None
            for k in range(terms):
                kind_0, kind_1 = kind_ref[k, 0], kind_ref[k, 1]
                flip_0, minus_0 = lax.rem(kind_0, 2), kind_0 // 2
                flip_1, minus_1 = lax.rem(kind_1, 2), kind_1 // 2
                from_s = s + flip_0 - 2 * s * flip_0
                from_t = t + flip_1 - 2 * t * flip_1
                sign = (1 - 2 * s * minus_0) * (1 - 2 * t * minus_1)
                value = g[k, PHYS * from_s + from_t] * sign.astype(F32).astype(BF16)
                product = matmul(value, rbuf[k])
                total = product if total is None else total + product
            partial = total.astype(BF16)

            @pl.when(has_outward)
            def _():
                arrived(n, 0, x).wait_recv()
                acc[n, x] = (partial.astype(F32) + recv[n, 0, x].astype(F32)).astype(BF16)

            @pl.when(jnp.logical_not(has_outward))
            def _():
                acc[n, x] = partial

            in_copy(n, x).start()
            return carry

        lax.fori_loop(0, pairs, right_pair, 0)

        def finish_pair(x, squares):
            arrived(n, 1, x).wait_recv()
            came_in = recv[n, 1, x].astype(F32)
            own = jnp.where(middle, 1.0, 0.0)
            whole = (came_in + own * acc[n, x].astype(F32)).astype(BF16)

            @pl.when(has_outward)
            def _():
                tot[n, x] = whole
                out_copy(n, x).start()

            value = two_site[x] - step_size * whole.astype(F32)
            two_site[x] = value
            if n < STEPS - 1:
                rounded = value.astype(BF16)
                for k in range(terms):
                    g[k, x] = matmul(envbuf[0, k], rounded).astype(BF16)
                return squares
            return squares + jnp.sum(value * value)

        squares = lax.fori_loop(0, pairs, finish_pair, jnp.zeros((), F32))

    size = two_site.shape[0] * two_site.shape[1] * two_site.shape[2]
    scale = lax.rsqrt(jnp.full((1, 1), squares, F32) / size + epsilon)

    def write_pair(x, carry):
        out_ref[x] = two_site[x] * scale
        return carry

    lax.fori_loop(0, pairs, write_pair, 0)

    iso_copy.wait_send()
    last_copy.wait_send()

    def drain_term(k, carry):
        env_copy(k).wait_send()

        @pl.when(is_odd)
        def _():
            fresh_copy(k).wait_send()

        return carry

    lax.fori_loop(0, terms, drain_term, 0)
    for n in range(STEPS):

        def drain_pair(x, carry):
            in_copy(n, x).wait_send()

            @pl.when(has_outward)
            def _():
                out_copy(n, x).wait_send()

            return carry

        lax.fori_loop(0, pairs, drain_pair, 0)


def shards(n_sec, n_term, meet_env, meet_iso, last_site, first_site, term_kind):
    terms, bond = meet_env.shape[1], meet_env.shape[2]
    pairs = PHYS * PHYS

    def by_level(site):
        return jnp.transpose(site[0], (1, 0, 2))

    vmem = pl.BlockSpec(memory_space=pltpu.VMEM)
    block = (bond, bond)
    dma = pltpu.SemaphoreType.DMA
    out = pl.pallas_call(
        functools.partial(kernel, n_sec, n_term, terms),
        out_shape=jax.ShapeDtypeStruct((pairs, bond, bond), F32),
        in_specs=[pl.BlockSpec(memory_space=pltpu.SMEM)] + [vmem] * 4,
        out_specs=vmem,
        scratch_shapes=[
            pltpu.VMEM((2, terms) + block, BF16),
            pltpu.VMEM((terms,) + block, BF16),
            pltpu.VMEM((terms,) + block, BF16),
            pltpu.VMEM((PHYS,) + block, BF16),
            pltpu.VMEM((PHYS,) + block, BF16),
            pltpu.VMEM((2, PHYS) + block, BF16),
            pltpu.VMEM((2, 3) + block, BF16),
            pltpu.VMEM((terms, pairs) + block, BF16),
            pltpu.VMEM((pairs,) + block, BF16),
            pltpu.VMEM((pairs,) + block, F32),
            pltpu.VMEM((STEPS, pairs) + block, BF16),
            pltpu.VMEM((STEPS, pairs) + block, BF16),
            pltpu.VMEM((STEPS, 2, pairs) + block, BF16),
            dma((2,)),
            dma((2,)),
            dma((terms,)),
            dma((terms,)),
            dma((terms,)),
            dma((terms,)),
            dma((STEPS, pairs)),
            dma((STEPS, 2, pairs)),
            dma((STEPS, pairs)),
        ],
        compiler_params=pltpu.CompilerParams(
            collective_id=0, has_side_effects=True, vmem_limit_bytes=48 * 1024 * 1024
        ),
    )(term_kind, meet_env[0], by_level(meet_iso), by_level(last_site), by_level(first_site))
    out = jnp.transpose(out, (1, 0, 2))
    return out.reshape(1, bond, PHYS, PHYS, bond)


def solution(mesh):
    in_specs = (
        P("sec", "term", None, None),
        P("sec", None, None, None),
        P("sec", None, None, None),
        P("sec", None, None, None),
        P("term", None),
    )
    out_specs = P("sec", None, None, None, None)
    body = functools.partial(shards, mesh.shape["sec"], mesh.shape["term"])
    return jax.shard_map(body, mesh=mesh, in_specs=in_specs, out_specs=out_specs, check_vma=False)
```

time: 149 us -> 59.7 us (0.40)
  waiting for transfers between devices: 84.3 us -> 0 us
  Pallas kernels: 0 us -> 55.7 us
  matrix products: 30.2 us -> 0 us
  between operations: 14.4 us -> 0.04 us
  local copies, waits for them, and re-layouts: 11.7 us -> 3.77 us
  other arithmetic: 4.21 us -> 0 us
  starting transfers between devices: 3.58 us -> 0 us
    psum x2 -> x0, waiting for transfers between devices: 76.7 us -> none  [shards(): lax.psum(partial_sum.astype(jnp.bfloat16), 'term').astype(jnp.float32)]
    pallas_call x0 -> x1, Pallas kernels: none -> 55.7 us  [shards(): pl.pallas_call(functools.partial(kernel, n_sec, n_term, terms), out_shape...]
    dot_general x12 -> x0, matrix products: 30.2 us -> none  [the longest x2 16.5 us: apply_local(): jnp.einsum('kaxc,kdc->axd', left_applied, right_env, preferred_element_ty...]
    ppermute x4 -> x0, waiting for transfers between devices: 7.63 us -> none  [the longest x2 7.62 us: shifted(): return lax.ppermute(block, axis, route)]
    ppermute x4 -> x0, starting transfers between devices: 3.32 us -> none  [the longest x2 3.21 us: swapped(): return lax.ppermute(value, axis, pairs)]
    reshape x5 -> x1, local copies, waits for them, and re-layouts: 4.17 us -> 1.78 us  [shards(): return out.reshape(1, bond, PHYS, PHYS, bond)]
    reduce_sum x1 -> x0, other arithmetic: 2.03 us -> none  [shards(): result = two_site * lax.rsqrt(jnp.mean(two_site * two_site) + epsilon)]
    ppermute x2 -> x0, local copies, waits for them, and re-layouts: 1.91 us -> none  [swapped(): return lax.ppermute(value, axis, pairs)]
  transfers between devices with their start and end apart: 6 -> 0, of which waited for: 3 -> 0; matrix products, arithmetic and copies ran while one was open for 13% -> 0% of each run, Pallas kernels for 0% -> 0%
where the time goes in v1:
time: 59.7 us; the launch traced here: 59.6 us
  Pallas kernels  55.7 us (93%)
  local copies, waits for them, and re-layouts  3.77 us (6%)
    pallas_call x1, Pallas kernels, shards(): pl.pallas_call(functools.partial(kernel, n_sec, n_term, terms), out_shape...  55.7 us
    unnamed x10, local copies, waits for them, and re-layouts  1.92 us
    reshape x1, local copies, waits for them, and re-layouts, shards(): return out.reshape(1, bond, PHYS, PHYS, bond)  1.78 us

profile of v1, /device:TPU:0, one launch (start us, length us, event | category | flops | bytes accessed | tf_op | source)
XLA Modules:
  0.0 59.6 jit_solution(15108295946508122770)
XLA Ops:
  0.0 0.0 copy-start.3
  0.0 0.0 copy-start.1
  0.0 0.0 copy-start.2
  0.0 0.7 %copy-done.3 = s32[6,2]{0,1:T(2,128)S(1)} copy-done((s32[6,2]{0,1:T(2,128)S(1)}, s32[6,2]{0,1:T(2,128)}, u32[]{:S(2)}) %copy-start.3) | copy-done | bytes 72
  0.7 0.1 copy.9.kind_ref
  0.8 0.0 copy-start
  0.8 1.1 %copy.14 = bf16[1,256,2,256]{3,1,2,0:T(8,128)(2,1)S(1)} copy(bf16[1,256,2,256]{3,2,1,0:T(2,128)(2,1)} %param.6) | data formatting | bytes 524288 | tf_op args[1]
  1.8 0.0 copy-done.1
  1.8 0.0 copy-done.2
  1.8 0.1 copy_bitcast_fusion
  1.9 0.1 copy-done
  2.0 55.7 %shard_map.55 = f32[4,256,256]{2,1,0:T(8,128)S(1)} custom-call(s32[6,2]{1,0:T(8,128)S(1)} %copy.9.kind_ref, bf16[6,256,256]{2,1,0:T(8,128)(2,1)S(1)} %bitcast.19, bf16[2,256,256]{2,1,0:T(8,128)(2,1)S(1)} %bitcast.18, bf16[2,256,256]{2,1,0:T(8,128)(2,1)S(1)} %get-tuple-element.6.last_ref, bf16[2,256,256]{2,1,0:T(8,128)(2,1)S(1)} %get-tuple-element.5.first_ref), custom_call_target="tpu_custom_call" | custom-call | tf_op jit(solution)/shard_map/pallas_call | solution.py:321
  57.8 1.8 %copy.10 = f32[1,256,2,2,256]{4,3,2,1,0:T(2,128)} copy(f32[1,256,2,2,256]{4,1,3,2,0:T(8,128)S(1)} %bitcast.17) | data formatting | bytes 2097152 | tf_op jit(solution)/shard_map/reshape | solution.py:355
Async XLA Ops:
  0.0 0.7 %copy-start.3 = (s32[6,2]{0,1:T(2,128)S(1)}, s32[6,2]{0,1:T(2,128)}, u32[]{:S(2)}) copy-start(s32[6,2]{0,1:T(2,128)} %param.9) | copy-start | bytes 148
  0.0 1.8 %copy-start.1 = (bf16[1,256,2,256]{3,2,1,0:T(2,128)(2,1)S(1)}, bf16[1,256,2,256]{3,2,1,0:T(2,128)(2,1)}, u32[]{:S(2)}) copy-start(bf16[1,256,2,256]{3,2,1,0:T(2,128)(2,1)} %param.8) | copy-start | bytes 786436
  0.0 1.8 %copy-start.2 = (bf16[1,256,2,256]{3,2,1,0:T(2,128)(2,1)S(1)}, bf16[1,256,2,256]{3,2,1,0:T(2,128)(2,1)}, u32[]{:S(2)}) copy-start(bf16[1,256,2,256]{3,2,1,0:T(2,128)(2,1)} %param.7) | copy-start | bytes 786436
  0.8 1.3 %copy-start = (bf16[1,6,256,256]{3,2,1,0:T(8,128)(2,1)S(1)}, bf16[1,6,256,256]{3,2,1,0:T(8,128)(2,1)}, u32[]{:S(2)}) copy-start(bf16[1,6,256,256]{3,2,1,0:T(8,128)(2,1)} %param.5) | copy-start | bytes 2359300

commit v2 on v1

--- a/solution.py
+++ b/solution.py
@@ -9,6 +9,8 @@
 
 PHYS = 2
 STEPS = 2
+PARTS = 4
+LAG = 5
 step_size = 0.2
 epsilon = 1e-06
 F32 = jnp.float32
@@ -213,64 +215,95 @@
 
         value = envbuf[0, k]
         for x in range(pairs):
-            g[k, x] = matmul(value, v[x]).astype(BF16)
+            g[0, k, x] = matmul(value, v[x]).astype(BF16)
         return carry
 
     lax.fori_loop(0, terms, left_term, 0)
 
+    rows = two_site.shape[1] // PARTS
+    chunks = pairs * PARTS
+
+    def partial_of(n, x):
+        s = x // PHYS
+        t = lax.rem(x, PHYS)
+        total = None
+        for k in range(terms):
+            kind_0, kind_1 = kind_ref[k, 0], kind_ref[k, 1]
+            flip_0, minus_0 = lax.rem(kind_0, 2), kind_0 // 2
+            flip_1, minus_1 = lax.rem(kind_1, 2), kind_1 // 2
+            from_s = s + flip_0 - 2 * s * flip_0
+            from_t = t + flip_1 - 2 * t * flip_1
+            sign = (1 - 2 * s * minus_0) * (1 - 2 * t * minus_1)
+            value = g[n, k, PHYS * from_s + from_t] * sign.astype(F32).astype(BF16)
+            product = matmul(value, rbuf[k])
+            total = product if total is None else total + product
+        total = total.astype(BF16)
+        for part in range(PARTS):
+            acc[n, PARTS * x + part] = total[part * rows : (part + 1) * rows]
+
+    def pass_inward(n, j):
+        @pl.when(has_outward)
+        def _():
+            arrived(n, 0, j).wait_recv()
+            acc[n, j] = (acc[n, j].astype(F32) + recv[n, 0, j].astype(F32)).astype(BF16)
+
+        in_copy(n, j).start()
+
+    def pass_outward(n, j, squares):
+        arrived(n, 1, j).wait_recv()
+        came_in = recv[n, 1, j].astype(F32)
+        own = jnp.where(middle, 1.0, 0.0)
+        whole = (came_in + own * acc[n, j].astype(F32)).astype(BF16)
+
+        @pl.when(has_outward)
+        def _():
+            tot[n, j] = whole
+            out_copy(n, j).start()
+
+        x = j // PARTS
+        span = pl.ds(pl.multiple_of(lax.rem(j, PARTS) * rows, rows), rows)
+        value = two_site[x, span] - step_size * whole.astype(F32)
+        two_site[x, span] = value
+        if n < STEPS - 1:
+            v[x, span] = value.astype(BF16)
+            return squares
+        return squares + jnp.sum(value * value)
+
+    def left_of(n, x):
+        for k in range(terms):
+            g[n, k, x] = matmul(envbuf[0, k], v[x]).astype(BF16)
+
+    zero = jnp.zeros((), F32)
     for n in range(STEPS):
 
-        def right_pair(x, carry):
-            s = x // PHYS
-            t = lax.rem(x, PHYS)
-            total = None
-            for k in range(terms):
-                kind_0, kind_1 = kind_ref[k, 0], kind_ref[k, 1]
-                flip_0, minus_0 = lax.rem(kind_0, 2), kind_0 // 2
-                flip_1, minus_1 = lax.rem(kind_1, 2), kind_1 // 2
-                from_s = s + flip_0 - 2 * s * flip_0
-                from_t = t + flip_1 - 2 * t * flip_1
-                sign = (1 - 2 * s * minus_0) * (1 - 2 * t * minus_1)
-                value = g[k, PHYS * from_s + from_t] * sign.astype(F32).astype(BF16)
-                product = matmul(value, rbuf[k])
-                total = product if total is None else total + product
-            partial = total.astype(BF16)
-
-            @pl.when(has_outward)
+        def step(j, squares):
+            @pl.when(jnp.logical_and(j < chunks, lax.rem(j, PARTS) == 0))
             def _():
-                arrived(n, 0, x).wait_recv()
-                acc[n, x] = (partial.astype(F32) + recv[n, 0, x].astype(F32)).astype(BF16)
-
-            @pl.when(jnp.logical_not(has_outward))
+                partial_of(n, j // PARTS)
+
+            @pl.when(j < chunks)
             def _():
-                acc[n, x] = partial
-
-            in_copy(n, x).start()
-            return carry
-
-        lax.fori_loop(0, pairs, right_pair, 0)
-
-        def finish_pair(x, squares):
-            arrived(n, 1, x).wait_recv()
-            came_in = recv[n, 1, x].astype(F32)
-            own = jnp.where(middle, 1.0, 0.0)
-            whole = (came_in + own * acc[n, x].astype(F32)).astype(BF16)
-
-            @pl.when(has_outward)
-            def _():
-                tot[n, x] = whole
-                out_copy(n, x).start()
-
-            value = two_site[x] - step_size * whole.astype(F32)
-            two_site[x] = value
+                pass_inward(n, j)
+
+            return squares
+
+        def head(j, squares):
+            return step(j, squares)
+
+        def body(j, squares):
+            squares = step(j, squares)
+            done = j - LAG
+            squares = pass_outward(n, done, squares)
             if n < STEPS - 1:
-                rounded = value.astype(BF16)
-                for k in range(terms):
-                    g[k, x] = matmul(envbuf[0, k], rounded).astype(BF16)
-                return squares
-            return squares + jnp.sum(value * value)
-
-        squares = lax.fori_loop(0, pairs, finish_pair, jnp.zeros((), F32))
+
+                @pl.when(lax.rem(done, PARTS) == PARTS - 1)
+                def _():
+                    left_of(n + 1, done // PARTS)
+
+            return squares
+
+        lax.fori_loop(0, LAG, head, 0)
+        squares = lax.fori_loop(LAG, chunks + LAG, body, zero)
 
     size = two_site.shape[0] * two_site.shape[1] * two_site.shape[2]
     scale = lax.rsqrt(jnp.full((1, 1), squares, F32) / size + epsilon)
@@ -296,7 +329,7 @@
     lax.fori_loop(0, terms, drain_term, 0)
     for n in range(STEPS):
 
-        def drain_pair(x, carry):
+        def drain_chunk(x, carry):
             in_copy(n, x).wait_send()
 
             @pl.when(has_outward)
@@ -305,7 +338,7 @@
 
             return carry
 
-        lax.fori_loop(0, pairs, drain_pair, 0)
+        lax.fori_loop(0, chunks, drain_chunk, 0)
 
 
 def shards(n_sec, n_term, meet_env, meet_iso, last_site, first_site, term_kind):
@@ -317,6 +350,8 @@
 
     vmem = pl.BlockSpec(memory_space=pltpu.VMEM)
     block = (bond, bond)
+    chunks = pairs * PARTS
+    strip = (bond // PARTS, bond)
     dma = pltpu.SemaphoreType.DMA
     out = pl.pallas_call(
         functools.partial(kernel, n_sec, n_term, terms),
@@ -331,21 +366,21 @@
             pltpu.VMEM((PHYS,) + block, BF16),
             pltpu.VMEM((2, PHYS) + block, BF16),
             pltpu.VMEM((2, 3) + block, BF16),
-            pltpu.VMEM((terms, pairs) + block, BF16),
+            pltpu.VMEM((STEPS, terms, pairs) + block, BF16),
             pltpu.VMEM((pairs,) + block, BF16),
             pltpu.VMEM((pairs,) + block, F32),
-            pltpu.VMEM((STEPS, pairs) + block, BF16),
-            pltpu.VMEM((STEPS, pairs) + block, BF16),
-            pltpu.VMEM((STEPS, 2, pairs) + block, BF16),
+            pltpu.VMEM((STEPS, chunks) + strip, BF16),
+            pltpu.VMEM((STEPS, chunks) + strip, BF16),
+            pltpu.VMEM((STEPS, 2, chunks) + strip, BF16),
             dma((2,)),
             dma((2,)),
             dma((terms,)),
             dma((terms,)),
             dma((terms,)),
             dma((terms,)),
-            dma((STEPS, pairs)),
-            dma((STEPS, 2, pairs)),
-            dma((STEPS, pairs)),
+            dma((STEPS, chunks)),
+            dma((STEPS, 2, chunks)),
+            dma((STEPS, chunks)),
         ],
         compiler_params=pltpu.CompilerParams(
             collective_id=0, has_side_effects=True, vmem_limit_bytes=48 * 1024 * 1024

time: 59.7 us -> 171 us (2.86)
  Pallas kernels: 55.7 us -> 167 us
    pallas_call x1, Pallas kernels: 55.7 us -> 167 us  [shards(): pl.pallas_call(functools.partial(kernel, n_sec, n_term, terms), out_shape...]
where the time goes in v2:
time: 171 us
  Pallas kernels  167 us (98%)
  local copies, waits for them, and re-layouts  3.77 us (2%)
    pallas_call x1, Pallas kernels, shards(): pl.pallas_call(functools.partial(kernel, n_sec, n_term, terms), out_shape...  167 us

profile of v2, /device:TPU:0, one launch (start us, length us, event | category | flops | bytes accessed | tf_op | source)
XLA Modules:
  0.0 170.7 jit_solution(7090210179366741734)
XLA Ops:
  0.0 0.0 copy-start.3
  0.0 0.0 copy-start.1
  0.0 0.0 copy-start.2
  0.0 0.7 copy-done.3
  0.7 0.1 copy.9.kind_ref
  0.8 0.0 copy-start
  0.8 1.1 copy.14
  1.8 0.0 copy-done.1
  1.8 0.0 copy-done.2
  1.8 0.1 copy_bitcast_fusion
  1.9 0.1 copy-done
  2.0 166.9 %shard_map.55 = f32[4,256,256]{2,1,0:T(8,128)S(1)} custom-call(s32[6,2]{1,0:T(8,128)S(1)} %copy.9.kind_ref, bf16[6,256,256]{2,1,0:T(8,128)(2,1)S(1)} %bitcast.19, bf16[2,256,256]{2,1,0:T(8,128)(2,1)S(1)} %bitcast.18, bf16[2,256,256]{2,1,0:T(8,128)(2,1)S(1)} %get-tuple-element.6.last_ref, bf16[2,256,256]{2,1,0:T(8,128)(2,1)S(1)} %get-tuple-element.5.first_ref), custom_call_target="tpu_custom_call" | custom-call | tf_op jit(solution)/shard_map/pallas_call | solution.py:356
  168.9 1.8 %copy.10 = f32[1,256,2,2,256]{4,3,2,1,0:T(2,128)} copy(f32[1,256,2,2,256]{4,1,3,2,0:T(8,128)S(1)} %bitcast.17) | data formatting | bytes 2097152 | tf_op jit(solution)/shard_map/reshape | solution.py:390
Async XLA Ops:
  0.0 0.7 copy-start.3
  0.0 1.8 %copy-start.1 = (bf16[1,256,2,256]{3,2,1,0:T(2,128)(2,1)S(1)}, bf16[1,256,2,256]{3,2,1,0:T(2,128)(2,1)}, u32[]{:S(2)}) copy-start(bf16[1,256,2,256]{3,2,1,0:T(2,128)(2,1)} %param.8) | copy-start | bytes 786436
  0.0 1.8 %copy-start.2 = (bf16[1,256,2,256]{3,2,1,0:T(2,128)(2,1)S(1)}, bf16[1,256,2,256]{3,2,1,0:T(2,128)(2,1)}, u32[]{:S(2)}) copy-start(bf16[1,256,2,256]{3,2,1,0:T(2,128)(2,1)} %param.7) | copy-start | bytes 786436
  0.8 1.3 copy-start

commit v3 on v2

--- a/solution.py
+++ b/solution.py
@@ -10,7 +10,8 @@
 PHYS = 2
 STEPS = 2
 PARTS = 4
-LAG = 5
+LAG = 6
+GROUP = 2
 step_size = 0.2
 epsilon = 1e-06
 F32 = jnp.float32
@@ -39,9 +40,10 @@
     came,
     basis,
     table,
-    g,
+    h,
     v,
     two_site,
+    early,
     acc,
     tot,
     recv,
@@ -175,31 +177,42 @@
     iso_copy.wait_recv()
     set_basis(0, piso)
 
-    def extend(value, which, kind):
-        first = jnp.where(kind == 1, 1, jnp.where(kind == 3, 2, 0))
-        second = jnp.where(kind == 0, 1, jnp.where(kind == 2, 2, 0))
-        wide_0 = matmul(value, basis[which, 0]).astype(BF16)
-        wide_1 = matmul(value, basis[which, 1]).astype(BF16)
-        result = matmul(table[which, first], wide_0) + matmul(table[which, second], wide_1)
-        return result.astype(BF16)
-
-    def extend_term(k, carry):
-        env_copy(k).wait_recv()
-        kind = kind_ref[k, 1 - odd]
-        value = extend(extend(envbuf[1 - odd, k], 0, kind), 1, kind)
+    def extend(values, which, kinds):
+        wide = [
+            [matmul(value, basis[which, r]).astype(BF16) for r in range(PHYS)] for value in values
+        ]
+        results = []
+        for (wide_0, wide_1), kind in zip(wide, kinds):
+            first = jnp.where(kind == 1, 1, jnp.where(kind == 3, 2, 0))
+            second = jnp.where(kind == 0, 1, jnp.where(kind == 2, 2, 0))
+            result = matmul(table[which, first], wide_0) + matmul(table[which, second], wide_1)
+            results.append(result.astype(BF16))
+        return results
+
+    group = GROUP if terms % GROUP == 0 else 1
+
+    def extend_group(i, carry):
+        members = [group * i + m for m in range(group)]
+        for k in members:
+            env_copy(k).wait_recv()
+        kinds = [kind_ref[k, 1 - odd] for k in members]
+        values = extend([envbuf[1 - odd, k] for k in members], 0, kinds)
+        values = extend(values, 1, kinds)
 
         @pl.when(is_odd)
         def _():
-            fresh[k] = value
-            fresh_copy(k).start()
+            for k, value in zip(members, values):
+                fresh[k] = value
+                fresh_copy(k).start()
 
         @pl.when(is_even)
         def _():
-            rbuf[k] = value.T
+            for k, value in zip(members, values):
+                rbuf[k] = value.T
 
         return carry
 
-    lax.fori_loop(0, terms, extend_term, 0)
+    lax.fori_loop(0, terms // group, extend_group, 0)
 
     last_copy.wait_recv()
     for s in range(PHYS):
@@ -208,38 +221,69 @@
             two_site[PHYS * s + t] = value
             v[PHYS * s + t] = value.astype(BF16)
 
-    def left_term(k, carry):
-        @pl.when(is_even)
-        def _():
+    def right_of(n, x):
+        value = v[x]
+        for k in range(terms):
+            h[n, k, x] = matmul(value, rbuf[k]).astype(BF16)
+
+    def first_right(x, carry):
+        right_of(0, x)
+        return carry
+
+    lax.fori_loop(0, pairs, first_right, 0)
+
+    def term_of(n, k, x):
+        s = x // PHYS
+        t = lax.rem(x, PHYS)
+        kind_0, kind_1 = kind_ref[k, 0], kind_ref[k, 1]
+        flip_0, minus_0 = lax.rem(kind_0, 2), kind_0 // 2
+        flip_1, minus_1 = lax.rem(kind_1, 2), kind_1 // 2
+        from_s = s + flip_0 - 2 * s * flip_0
+        from_t = t + flip_1 - 2 * t * flip_1
+        sign = (1 - 2 * s * minus_0) * (1 - 2 * t * minus_1)
+        value = h[n, k, PHYS * from_s + from_t] * sign.astype(F32).astype(BF16)
+        return matmul(envbuf[0, k], value)
+
+    @pl.when(is_even)
+    def _():
+        for x in range(pairs):
+            early[x] = jnp.zeros(early.shape[1:], F32)
+
+        def early_term(k, carry):
             fresh_copy(k).wait_recv()
-
-        value = envbuf[0, k]
-        for x in range(pairs):
-            g[0, k, x] = matmul(value, v[x]).astype(BF16)
-        return carry
-
-    lax.fori_loop(0, terms, left_term, 0)
+            for x in range(pairs):
+                early[x] += term_of(0, k, x)
+            return carry
+
+        lax.fori_loop(0, terms - 1, early_term, 0)
+        fresh_copy(terms - 1).wait_recv()
 
     rows = two_site.shape[1] // PARTS
     chunks = pairs * PARTS
 
-    def partial_of(n, x):
-        s = x // PHYS
-        t = lax.rem(x, PHYS)
-        total = None
-        for k in range(terms):
-            kind_0, kind_1 = kind_ref[k, 0], kind_ref[k, 1]
-            flip_0, minus_0 = lax.rem(kind_0, 2), kind_0 // 2
-            flip_1, minus_1 = lax.rem(kind_1, 2), kind_1 // 2
-            from_s = s + flip_0 - 2 * s * flip_0
-            from_t = t + flip_1 - 2 * t * flip_1
-            sign = (1 - 2 * s * minus_0) * (1 - 2 * t * minus_1)
-            value = g[n, k, PHYS * from_s + from_t] * sign.astype(F32).astype(BF16)
-            product = matmul(value, rbuf[k])
-            total = product if total is None else total + product
+    def put_partial(n, x, total):
         total = total.astype(BF16)
         for part in range(PARTS):
             acc[n, PARTS * x + part] = total[part * rows : (part + 1) * rows]
+
+    def full_partial(n, x):
+        total = term_of(n, 0, x)
+        for k in range(1, terms):
+            total = total + term_of(n, k, x)
+        put_partial(n, x, total)
+
+    def partial_of(n, x):
+        if n > 0:
+            full_partial(n, x)
+            return
+
+        @pl.when(is_odd)
+        def _():
+            full_partial(n, x)
+
+        @pl.when(is_even)
+        def _():
+            put_partial(n, x, early[x] + term_of(n, terms - 1, x))
 
     def pass_inward(n, j):
         @pl.when(has_outward)
@@ -269,10 +313,7 @@
             return squares
         return squares + jnp.sum(value * value)
 
-    def left_of(n, x):
-        for k in range(terms):
-            g[n, k, x] = matmul(envbuf[0, k], v[x]).astype(BF16)
-
+    lag = jnp.where(has_outward, min(LAG, chunks), chunks)
     zero = jnp.zeros((), F32)
     for n in range(STEPS):
 
@@ -292,27 +333,31 @@
 
         def body(j, squares):
             squares = step(j, squares)
-            done = j - LAG
+            done = j - lag
             squares = pass_outward(n, done, squares)
             if n < STEPS - 1:
 
                 @pl.when(lax.rem(done, PARTS) == PARTS - 1)
                 def _():
-                    left_of(n + 1, done // PARTS)
+                    right_of(n + 1, done // PARTS)
 
             return squares
 
-        lax.fori_loop(0, LAG, head, 0)
-        squares = lax.fori_loop(LAG, chunks + LAG, body, zero)
+        lax.fori_loop(0, lag, head, 0)
+        squares = lax.fori_loop(lag, chunks + lag, body, zero)
 
     size = two_site.shape[0] * two_site.shape[1] * two_site.shape[2]
     scale = lax.rsqrt(jnp.full((1, 1), squares, F32) / size + epsilon)
 
-    def write_pair(x, carry):
-        out_ref[x] = two_site[x] * scale
-        return carry
-
-    lax.fori_loop(0, pairs, write_pair, 0)
+    lanes = out_ref.shape[1]
+    halves = two_site.shape[2] // lanes
+    stride = PHYS * PHYS * halves
+    for s in range(PHYS):
+        for t in range(PHYS):
+            for c in range(halves):
+                span = pl.ds((s * halves + c) * PHYS + t, two_site.shape[1], stride=stride)
+                columns = pl.ds(c * lanes, lanes)
+                out_ref[span, :] = two_site[PHYS * s + t, :, columns] * scale
 
     iso_copy.wait_send()
     last_copy.wait_send()
@@ -352,10 +397,11 @@
     block = (bond, bond)
     chunks = pairs * PARTS
     strip = (bond // PARTS, bond)
+    lanes = min(bond, 128)
     dma = pltpu.SemaphoreType.DMA
     out = pl.pallas_call(
         functools.partial(kernel, n_sec, n_term, terms),
-        out_shape=jax.ShapeDtypeStruct((pairs, bond, bond), F32),
+        out_shape=jax.ShapeDtypeStruct((pairs * bond * bond // lanes, lanes), F32),
         in_specs=[pl.BlockSpec(memory_space=pltpu.SMEM)] + [vmem] * 4,
         out_specs=vmem,
         scratch_shapes=[
@@ -368,6 +414,7 @@
             pltpu.VMEM((2, 3) + block, BF16),
             pltpu.VMEM((STEPS, terms, pairs) + block, BF16),
             pltpu.VMEM((pairs,) + block, BF16),
+            pltpu.VMEM((pairs,) + block, F32),
             pltpu.VMEM((pairs,) + block, F32),
             pltpu.VMEM((STEPS, chunks) + strip, BF16),
             pltpu.VMEM((STEPS, chunks) + strip, BF16),
@@ -386,7 +433,8 @@
             collective_id=0, has_side_effects=True, vmem_limit_bytes=48 * 1024 * 1024
         ),
     )(term_kind, meet_env[0], by_level(meet_iso), by_level(last_site), by_level(first_site))
-    out = jnp.transpose(out, (1, 0, 2))
+    out = out.reshape(bond, PHYS, bond // lanes, PHYS, lanes)
+    out = jnp.transpose(out, (0, 1, 3, 2, 4))
     return out.reshape(1, bond, PHYS, PHYS, bond)
 
 

time: 171 us -> 57.3 us (0.34)
  Pallas kernels: 167 us -> 54.1 us
    pallas_call x1, Pallas kernels: 167 us -> 54.1 us  [shards(): pl.pallas_call(functools.partial(kernel, n_sec, n_term, terms), out_shape...]
    reshape x1 -> x0, local copies, waits for them, and re-layouts: 1.78 us -> none  [shards(): return out.reshape(1, bond, PHYS, PHYS, bond)]
where the time goes in v3:
time: 57.3 us; the launch traced here: 57.1 us
  Pallas kernels  54.1 us (94%)
  local copies, waits for them, and re-layouts  2.97 us (5%)
    pallas_call x1, Pallas kernels, shards(): pl.pallas_call(functools.partial(kernel, n_sec, n_term, terms), out_shape...  54.1 us
    unnamed x11, local copies, waits for them, and re-layouts  2.89 us

profile of v3, /device:TPU:0, one launch (start us, length us, event | category | flops | bytes accessed | tf_op | source)
XLA Modules:
  0.0 57.1 jit_solution(678571269378178551)
XLA Ops:
  0.0 0.0 copy-start.3
  0.0 0.0 copy-start.1
  0.0 0.0 copy-start.2
  0.0 0.7 %copy-done.3 = s32[6,2]{0,1:T(2,128)S(1)} copy-done((s32[6,2]{0,1:T(2,128)S(1)}, s32[6,2]{0,1:T(2,128)}, u32[]{:S(2)}) %copy-start.3) | copy-done | bytes 72
  0.7 0.1 copy.9.kind_ref
  0.8 0.0 copy-start
  0.8 1.1 %copy.14 = bf16[1,256,2,256]{3,1,2,0:T(8,128)(2,1)S(1)} copy(bf16[1,256,2,256]{3,2,1,0:T(2,128)(2,1)} %param.6) | data formatting | bytes 524288 | tf_op args[1]
  1.8 0.0 copy-done.1
  1.8 0.0 copy-done.2
  1.8 0.1 copy_bitcast_fusion
  1.9 0.1 copy-done
  2.0 54.1 %shard_map.55 = f32[2048,128]{1,0:T(8,128)S(1)} custom-call(s32[6,2]{1,0:T(8,128)S(1)} %copy.9.kind_ref, bf16[6,256,256]{2,1,0:T(8,128)(2,1)S(1)} %bitcast.21, bf16[2,256,256]{2,1,0:T(8,128)(2,1)S(1)} %bitcast.20, bf16[2,256,256]{2,1,0:T(8,128)(2,1)S(1)} %get-tuple-element.6.last_ref, bf16[2,256,256]{2,1,0:T(8,128)(2,1)S(1)} %get-tuple-element.5.first_ref), custom_call_target="tpu_custom_call" | custom-call | tf_op jit(solution)/shard_map/pallas_call | solution.py:402
  56.1 1.0 %copy.16 = f32[1,256,2,2,256]{4,3,2,1,0:T(2,128)} copy(f32[1,256,2,2,256]{4,3,2,1,0:T(2,128)S(1)} %bitcast.19) | data formatting | bytes 2097152
Async XLA Ops:
  0.0 0.7 %copy-start.3 = (s32[6,2]{0,1:T(2,128)S(1)}, s32[6,2]{0,1:T(2,128)}, u32[]{:S(2)}) copy-start(s32[6,2]{0,1:T(2,128)} %param.9) | copy-start | bytes 148
  0.0 1.8 %copy-start.1 = (bf16[1,256,2,256]{3,2,1,0:T(2,128)(2,1)S(1)}, bf16[1,256,2,256]{3,2,1,0:T(2,128)(2,1)}, u32[]{:S(2)}) copy-start(bf16[1,256,2,256]{3,2,1,0:T(2,128)(2,1)} %param.8) | copy-start | bytes 786436
  0.0 1.8 %copy-start.2 = (bf16[1,256,2,256]{3,2,1,0:T(2,128)(2,1)S(1)}, bf16[1,256,2,256]{3,2,1,0:T(2,128)(2,1)}, u32[]{:S(2)}) copy-start(bf16[1,256,2,256]{3,2,1,0:T(2,128)(2,1)} %param.7) | copy-start | bytes 786436
  0.8 1.3 %copy-start = (bf16[1,6,256,256]{3,2,1,0:T(8,128)(2,1)S(1)}, bf16[1,6,256,256]{3,2,1,0:T(8,128)(2,1)}, u32[]{:S(2)}) copy-start(bf16[1,6,256,256]{3,2,1,0:T(8,128)(2,1)} %param.5) | copy-start | bytes 2359300

commit v4 on v3

--- a/solution.py
+++ b/solution.py
@@ -10,7 +10,7 @@
 PHYS = 2
 STEPS = 2
 PARTS = 4
-LAG = 6
+LAG = 9
 GROUP = 2
 step_size = 0.2
 epsilon = 1e-06
@@ -311,10 +311,10 @@
         if n < STEPS - 1:
             v[x, span] = value.astype(BF16)
             return squares
-        return squares + jnp.sum(value * value)
+        return squares + jnp.sum((value * value).reshape((rows // 8, 8, value.shape[1])), axis=0)
 
     lag = jnp.where(has_outward, min(LAG, chunks), chunks)
-    zero = jnp.zeros((), F32)
+    zero = jnp.zeros((8, two_site.shape[2]), F32)
     for n in range(STEPS):
 
         def step(j, squares):
@@ -347,7 +347,7 @@
         squares = lax.fori_loop(lag, chunks + lag, body, zero)
 
     size = two_site.shape[0] * two_site.shape[1] * two_site.shape[2]
-    scale = lax.rsqrt(jnp.full((1, 1), squares, F32) / size + epsilon)
+    scale = lax.rsqrt(jnp.full((1, 1), jnp.sum(squares), F32) / size + epsilon)
 
     lanes = out_ref.shape[1]
     halves = two_site.shape[2] // lanes

time: 57.3 us -> 54.1 us (0.944)
  Pallas kernels: 54.1 us -> 50.9 us
    pallas_call x1, Pallas kernels: 54.1 us -> 50.9 us  [shards(): pl.pallas_call(functools.partial(kernel, n_sec, n_term, terms), out_shape...]
where the time goes in v4:
time: 54.1 us; the launch traced here: 53.9 us
  Pallas kernels  50.9 us (94%)
  local copies, waits for them, and re-layouts  2.97 us (5%)
    pallas_call x1, Pallas kernels, shards(): pl.pallas_call(functools.partial(kernel, n_sec, n_term, terms), out_shape...  50.9 us
    unnamed x11, local copies, waits for them, and re-layouts  2.89 us

profile of v4, /device:TPU:0, one launch (start us, length us, event | category | flops | bytes accessed | tf_op | source)
XLA Modules:
  0.0 53.9 jit_solution(5011659342228483533)
XLA Ops:
  0.0 0.0 copy-start.3
  0.0 0.0 copy-start.1
  0.0 0.0 copy-start.2
  0.0 0.7 %copy-done.3 = s32[6,2]{0,1:T(2,128)S(1)} copy-done((s32[6,2]{0,1:T(2,128)S(1)}, s32[6,2]{0,1:T(2,128)}, u32[]{:S(2)}) %copy-start.3) | copy-done | bytes 72
  0.7 0.1 copy.9.kind_ref
  0.8 0.0 copy-start
  0.8 1.1 %copy.14 = bf16[1,256,2,256]{3,1,2,0:T(8,128)(2,1)S(1)} copy(bf16[1,256,2,256]{3,2,1,0:T(2,128)(2,1)} %param.6) | data formatting | bytes 524288 | tf_op args[1]
  1.8 0.0 copy-done.1
  1.8 0.0 copy-done.2
  1.8 0.1 copy_bitcast_fusion
  1.9 0.1 copy-done
  2.0 50.9 %shard_map.55 = f32[2048,128]{1,0:T(8,128)S(1)} custom-call(s32[6,2]{1,0:T(8,128)S(1)} %copy.9.kind_ref, bf16[6,256,256]{2,1,0:T(8,128)(2,1)S(1)} %bitcast.21, bf16[2,256,256]{2,1,0:T(8,128)(2,1)S(1)} %bitcast.20, bf16[2,256,256]{2,1,0:T(8,128)(2,1)S(1)} %get-tuple-element.6.last_ref, bf16[2,256,256]{2,1,0:T(8,128)(2,1)S(1)} %get-tuple-element.5.first_ref), custom_call_target="tpu_custom_call" | custom-call | tf_op jit(solution)/shard_map/pallas_call | solution.py:402
  52.9 1.0 %copy.16 = f32[1,256,2,2,256]{4,3,2,1,0:T(2,128)} copy(f32[1,256,2,2,256]{4,3,2,1,0:T(2,128)S(1)} %bitcast.19) | data formatting | bytes 2097152
Async XLA Ops:
  0.0 0.7 %copy-start.3 = (s32[6,2]{0,1:T(2,128)S(1)}, s32[6,2]{0,1:T(2,128)}, u32[]{:S(2)}) copy-start(s32[6,2]{0,1:T(2,128)} %param.9) | copy-start | bytes 148
  0.0 1.8 %copy-start.1 = (bf16[1,256,2,256]{3,2,1,0:T(2,128)(2,1)S(1)}, bf16[1,256,2,256]{3,2,1,0:T(2,128)(2,1)}, u32[]{:S(2)}) copy-start(bf16[1,256,2,256]{3,2,1,0:T(2,128)(2,1)} %param.8) | copy-start | bytes 786436
  0.0 1.8 %copy-start.2 = (bf16[1,256,2,256]{3,2,1,0:T(2,128)(2,1)S(1)}, bf16[1,256,2,256]{3,2,1,0:T(2,128)(2,1)}, u32[]{:S(2)}) copy-start(bf16[1,256,2,256]{3,2,1,0:T(2,128)(2,1)} %param.7) | copy-start | bytes 786436
  0.8 1.3 %copy-start = (bf16[1,6,256,256]{3,2,1,0:T(8,128)(2,1)S(1)}, bf16[1,6,256,256]{3,2,1,0:T(8,128)(2,1)}, u32[]{:S(2)}) copy-start(bf16[1,6,256,256]{3,2,1,0:T(8,128)(2,1)} %param.5) | copy-start | bytes 2359300
